TPU v7x, 128 devices: a whole 4x4x4 slice. The times are simulated.
128 devices in a mesh: req: 16 (over z, y), mlp: 8 (over x, core).
Axes of the slice: x: 4, y: 4, z: 4, core: 2. Of those that a mesh axis runs over, the one named last changes fastest.
Arguments:
- hidden: bfloat16 [8192, 3584], P('req', 'mlp'), may hold values from -6 to 6
- query_heads: bfloat16 [8192, 3584], P('req', 'mlp'), may hold values from -4 to 4
- key_heads: bfloat16 [8192, 3584], P('req', 'mlp'), may hold values from -4 to 4
- value_heads: bfloat16 [8192, 3584], P('req', 'mlp'), may hold values from -6 to 6
- segment_ids: int32 [8192], P('req'), may hold values from 0 to 63, never falling along the last dimension, each value on 1 to 1024 neighbouring positions
- page_table: int32 [16, 32], P('req'), may hold values from 0 to 31, each once within a row
- mamba_conv_input: bfloat16 [8192, 7168], P('req', 'mlp'), may hold values from -6 to 6
- mamba_output_gate: bfloat16 [8192, 7168], P('req', 'mlp'), may hold values from -6 to 6
- state_input_projection: bfloat16 [8192, 128], P('req'), may hold values from -6 to 6
- state_output_projection: bfloat16 [8192, 128], P('req'), may hold values from -6 to 6
- discrete_step_size: float32 [8192, 112], P('req', 'mlp'), may hold values from 0.24 to 100, as said below
- head_decay_rate: float32 [112], P('mlp'), may hold values from 0.00024414062 to 0.05, as said below
- skip_gain: float32 [112], P('mlp'), may hold values from 0.5 to 2
- mamba_gated_norm_gain: float32 [7168], P('mlp'), may hold values from 0.1 to 1.9
- attn_proj: bfloat16 [3584, 3584], P('mlp'), may hold values from -0.09375 to 0.09375
- mamba_output_projection: bfloat16 [7168, 3584], P('mlp'), may hold values from -0.0625 to 0.0625
- mlp_norm_gain: float32 [3584], replicated, may hold values from 0.1 to 1.9
- gate_proj: bfloat16 [3584, 7168], P('req', 'mlp'), may hold values from -0.09375 to 0.09375
- up_proj: bfloat16 [3584, 7168], P('req', 'mlp'), may hold values from -0.09375 to 0.09375
- down_proj: bfloat16 [7168, 3584], P('mlp', 'req'), may hold values from -0.0625 to 0.0625
- next_norm_gain: float32 [3584], P('mlp'), may hold values from 0.1 to 1.9
Outputs:
- new_hidden: bfloat16 [8192, 3584], P('req', 'mlp')
- next_normed: bfloat16 [8192, 3584], P('req', 'mlp')
- kv_cache: bfloat16 [2, 16, 512, 3584], P(None, 'mlp', 'req')
Inputs may be any that keep to these rules, and one draw needn't show every extreme that they name: `segment_ids`: prompt ids never fall along the stream; a prompt has 1 to 1024 tokens and one has exactly 1024. `page_table`: each request group's row names every page of its pool once. `discrete_step_size`: Positive. `head_decay_rate`: Positive.
All inputs are finite; a program needn't handle non-finite values.
Results may differ from a plain program's by a relative error of at most 0.006.
Values may be sent and summed in bfloat16 or wider, within the bound.
No kernel may reach another device: no remote copies, remote signals or barrier semaphores. Data moves between devices by JAX's collectives and lax.ppermute only.
A program may use at most 128 MiB of HBM per device.

v0:
```python
import math
import jax
import jax.numpy as jnp
from jax import lax
from jax.sharding import PartitionSpec as P

HD = 224
MAMBA_HEAD_COUNT = 112
MAMBA_HEAD_SIZE = 64
STATE_SIZE = 64
STATE_GROUPS = 2
REACH = 2
PAGE = 16
EPSILON = 1e-05
exact_mode = lax.Precision.HIGHEST


def from_behind(value, axis, steps):
    count = lax.axis_size(axis)
    leading, last = (max(0, -steps), min(count, count - steps))
    return lax.ppermute(value, axis, [(source, source + steps) for source in range(leading, last)])


def entering(x, axis, combine, identity):
    devices, mine = (lax.axis_size(axis), lax.axis_index(axis))
    everything = jax.tree.map(lambda part: lax.all_gather(part, axis), x)
    start = jax.tree.map(
        lambda part, zero: jnp.broadcast_to(jnp.asarray(zero, part.dtype), part.shape), x, identity
    )

    def step(k, before):
        reached = k < mine
        new = combine(before, jax.tree.map(lambda part: part[k], everything))
        return jax.tree.map(lambda a, b: jnp.where(reached, a, b), new, before)

    return lax.fori_loop(0, devices, step, start)


def attend_rows(
    query_rows, segment_rows, pos_rows, all_keys, all_values, key_segs, key_pos, head_count
):
    row_total = query_rows.shape[0]
    key_total = all_keys.shape[0]
    query_split = query_rows.reshape(row_total, head_count, HD)
    key_split = all_keys.reshape(key_total, head_count, HD)
    value_split = all_values.reshape(key_total, head_count, HD)
    scores = jnp.einsum(
        "qhd,khd->hqk", query_split, key_split, preferred_element_type=jnp.float32
    ) * (1.0 / math.sqrt(HD))
    allowed = (segment_rows[:, None] == key_segs[None, :]) & (key_pos[None, :] <= pos_rows[:, None])
    scores = jnp.where(allowed[None, :, :], scores, -jnp.inf)
    top_score = jnp.max(scores, axis=2, keepdims=True)
    raised = jnp.exp(scores - top_score)
    weights = (raised / jnp.sum(raised, axis=2, keepdims=True)).astype(jnp.bfloat16)
    summed = jnp.einsum("hqk,khd->qhd", weights, value_split, preferred_element_type=jnp.float32)
    return summed.astype(jnp.bfloat16).reshape(row_total, head_count * HD)


def block_contributions(
    input_token_rows,
    input_proj_rows,
    output_proj_rows,
    step_size_rows,
    head_decay_rate,
    segment_rows,
    segment_prior_state,
    group_index,
    head_width,
):
    row_count = input_token_rows.shape[0]
    head_count = step_size_rows.shape[1]
    input_float = input_token_rows.astype(jnp.float32).reshape(row_count, head_count, head_width)
    b_float = input_proj_rows.astype(jnp.float32)
    c_float = output_proj_rows.astype(jnp.float32)
    running = jnp.cumsum(-step_size_rows * head_decay_rate[None, :], axis=0)
    positions = jnp.arange(row_count, dtype=jnp.int32)
    live = (segment_rows[:, None] == segment_rows[None, :]) & (
        positions[:, None] >= positions[None, :]
    )
    spread = running.T[:, :, None] - running.T[:, None, :]
    mixing = jnp.exp(jnp.where(live[None, :, :], spread, -1e30))
    inner = jnp.einsum("tgn,ugn->gtu", c_float, b_float, precision=exact_mode)
    driven = input_float * step_size_rows[:, :, None]
    local_output = jnp.einsum(
        "htu,uhp->thp", mixing * inner[group_index], driven, precision=exact_mode
    )
    b_per_head = b_float[:, group_index, :]
    output_proj_per_head = c_float[:, group_index, :]
    tail_rows = segment_rows == segment_rows[row_count - 1]
    tail_gain = jnp.where(
        tail_rows[:, None], jnp.exp(running[row_count - 1][None, :] - running), 0.0
    )
    state_local_part = jnp.einsum(
        "uh,uhp,uhn->hpn", tail_gain, driven, b_per_head, precision=exact_mode
    )
    decay_cumulative = jnp.where(
        segment_rows[row_count - 1] == segment_prior_state, jnp.exp(running[row_count - 1]), 0.0
    )
    entry_weighting = jnp.where(
        (segment_rows == segment_prior_state)[:, None], jnp.exp(running), 0.0
    )
    return (
        local_output,
        decay_cumulative,
        state_local_part,
        entry_weighting,
        input_float,
        output_proj_per_head,
    )


def finish(local_output, entry_weighting, input_float, output_proj_per_head, carry_in, skip_gain):
    carried = jnp.einsum("hpn,thn->thp", carry_in, output_proj_per_head, precision=exact_mode)
    result = (
        local_output
        + entry_weighting[:, :, None] * carried
        + skip_gain[None, :, None] * input_float
    )
    return result.reshape(result.shape[0], result.shape[1] * result.shape[2])


def merge_states(earlier, later):
    decay_early, state_early = earlier
    decay_late, state_late = later
    return (decay_early * decay_late, decay_late[:, None, None] * state_early + state_late)


def body(
    hidden,
    query_heads,
    key_heads,
    value_heads,
    segment_ids,
    page_table,
    mamba_conv_input,
    mamba_output_gate,
    state_input_projection,
    state_output_projection,
    discrete_step_size,
    head_decay_rate,
    skip_gain,
    mamba_gated_norm_gain,
    attn_proj,
    mamba_output_projection,
    mlp_norm_gain,
    gate_proj,
    up_proj,
    down_proj,
    next_norm_gain,
):
    row_count = query_heads.shape[0]
    head_count = query_heads.shape[1] // HD
    lane_count = hidden.shape[1]
    owner_index = lax.axis_index("req")
    column = lax.axis_index("mlp")
    first_row = owner_index * row_count
    lead_rows = REACH * row_count
    shifted_ids = segment_ids + 1
    key_parts = []
    value_parts = []
    segment_parts = []
    for distance in range(REACH, 0, -1):
        moved_ids = from_behind(shifted_ids, "req", distance)
        segment_parts.append(moved_ids - 1)
        moved_keys, moved_values = from_behind((key_heads, value_heads), "req", distance)
        key_parts.append(moved_keys)
        value_parts.append(moved_values)
    key_segs = jnp.concatenate(segment_parts + [segment_ids], axis=0)
    key_pos = first_row - lead_rows + jnp.arange(lead_rows + row_count, dtype=jnp.int32)
    segment_prior_state = segment_parts[-1][row_count - 1]
    all_keys = jnp.concatenate(key_parts + [key_heads], axis=0)
    all_values = jnp.concatenate(value_parts + [value_heads], axis=0)
    block_rows = min(row_count, 512)

    def one_block(block_index):
        first_local = block_index * block_rows
        pos_rows = first_row + first_local + jnp.arange(block_rows, dtype=jnp.int32)
        return attend_rows(
            query_heads, segment_ids, pos_rows, all_keys, all_values, key_segs, key_pos, head_count
        )

    attended = lax.map(one_block, jnp.arange(row_count // block_rows, dtype=jnp.int32)).reshape(
        row_count, head_count * HD
    )
    page_count = page_table.shape[1]
    key_pages = (
        key_heads.reshape(page_count, PAGE, head_count, HD)
        .transpose(2, 0, 1, 3)
        .reshape(head_count, page_count, PAGE * HD)
    )
    value_pages = (
        value_heads.reshape(page_count, PAGE, head_count, HD)
        .transpose(2, 0, 1, 3)
        .reshape(head_count, page_count, PAGE * HD)
    )
    stacked = jnp.stack([key_pages, value_pages])
    kv_cache = jnp.zeros_like(stacked).at[:, :, page_table[0]].set(stacked)
    mamba_heads = discrete_step_size.shape[1]
    group_values = MAMBA_HEAD_COUNT // STATE_GROUPS
    b_groups = state_input_projection.reshape(row_count, STATE_GROUPS, STATE_SIZE)
    c_groups = state_output_projection.reshape(row_count, STATE_GROUPS, STATE_SIZE)
    group_index = jnp.arange(mamba_heads, dtype=jnp.int32) % STATE_GROUPS
    (
        local_output,
        decay_cumulative,
        state_local_part,
        entry_weighting,
        input_float,
        output_proj_per_head,
    ) = block_contributions(
        mamba_conv_input,
        b_groups,
        c_groups,
        discrete_step_size,
        head_decay_rate,
        segment_ids,
        segment_prior_state,
        group_index,
        MAMBA_HEAD_SIZE,
    )
    unused_decay, carry_in = entering(
        (decay_cumulative, state_local_part),
        "req",
        merge_states,
        (jnp.ones_like(decay_cumulative), jnp.zeros_like(state_local_part)),
    )
    mamba_output = finish(
        local_output, entry_weighting, input_float, output_proj_per_head, carry_in, skip_gain
    )
    gated_output = mamba_output * jax.nn.silu(mamba_output_gate.astype(jnp.float32))
    grouped_values = gated_output.reshape(
        row_count, mamba_heads // STATE_GROUPS, STATE_GROUPS, MAMBA_HEAD_SIZE
    )
    group_squares = jnp.sum(grouped_values * grouped_values, axis=(1, 3))
    running_totals = lax.psum(group_squares, "mlp")
    inverse_group = lax.rsqrt(running_totals / (group_values * MAMBA_HEAD_SIZE) + EPSILON)
    mnormed = (
        (grouped_values * inverse_group[:, None, :, None]).reshape(
            row_count, mamba_heads * MAMBA_HEAD_SIZE
        )
        * mamba_gated_norm_gain[None, :]
    ).astype(jnp.bfloat16)
    projected = jnp.dot(attended, attn_proj, preferred_element_type=jnp.float32) + jnp.dot(
        mnormed, mamba_output_projection, preferred_element_type=jnp.float32
    )
    width_total = projected.shape[1]
    offset = column * lane_count
    own_part = lax.dynamic_slice_in_dim(projected, offset, lane_count, 1) + hidden.astype(
        jnp.float32
    )
    mixed_rows = lax.psum(lax.dynamic_update_slice_in_dim(projected, own_part, offset, 1), "mlp")
    mixed_share = lax.dynamic_slice_in_dim(mixed_rows, offset, lane_count, 1)
    inverse_root_mean = lax.rsqrt(jnp.mean(mixed_rows * mixed_rows, axis=1) + EPSILON)
    normed = (mixed_rows * inverse_root_mean[:, None] * mlp_norm_gain[None, :]).astype(jnp.bfloat16)
    gate_act = jnp.dot(
        normed,
        lax.all_gather(gate_proj, "req", axis=0, tiled=True),
        preferred_element_type=jnp.float32,
    )
    up_act = jnp.dot(
        normed,
        lax.all_gather(up_proj, "req", axis=0, tiled=True),
        preferred_element_type=jnp.float32,
    )
    latent_activation = (jax.nn.silu(gate_act) * up_act).astype(jnp.bfloat16)
    partial_value = jnp.dot(
        latent_activation,
        lax.all_gather(down_proj, "req", axis=1, tiled=True),
        preferred_element_type=jnp.float32,
    )
    mlp_share = lax.psum_scatter(partial_value, "mlp", scatter_dimension=1, tiled=True)
    new_hidden = (mixed_share + mlp_share).astype(jnp.bfloat16)
    widened = new_hidden.astype(jnp.float32)
    total_sq = lax.psum(jnp.sum(widened * widened, axis=1), "mlp")
    next_normed = (
        widened * lax.rsqrt(total_sq / width_total + EPSILON)[:, None] * next_norm_gain[None, :]
    ).astype(jnp.bfloat16)
    return (new_hidden, next_normed, kv_cache)


def solution(mesh):
    return jax.shard_map(
        body,
        mesh=mesh,
        in_specs=(
            P("req", "mlp"),
            P("req", "mlp"),
            P("req", "mlp"),
            P("req", "mlp"),
            P("req"),
            P("req", None),
            P("req", "mlp"),
            P("req", "mlp"),
            P("req", None),
            P("req", None),
            P("req", "mlp"),
            P("mlp"),
            P("mlp"),
            P("mlp"),
            P("mlp", None),
            P("mlp", None),
            P(),
            P("req", "mlp"),
            P("req", "mlp"),
            P("mlp", "req"),
            P("mlp"),
        ),
        out_specs=(P("req", "mlp"), P("req", "mlp"), P(None, "mlp", "req", None)),
        check_vma=False,
    )
```

profile of v0, /device:TPU:0, one launch (start us, length us, event | category | flops | bytes accessed | tf_op | source)
XLA Modules:
  0.0 616.1 jit_solution(2052999723825984348)
XLA Ops:
  8.7 3.6 collective-permute-start.3
  25.6 3.5 fusion.22
  29.2 5.4 collective-permute-start.2
  34.6 4.1 collective-permute-start.4
  38.7 4.3 collective-permute-start.5
  43.0 4.0 collective-permute-start
  47.0 3.6 collective-permute-start.1
  56.1 8.8 %gather_fusion = f32[14,512,512]{2,1,0:T(8,128)} fusion(f32[2,512,512]{2,1,0:T(8,128)} %fusion.59, s32[1024]{0:T(1024)} %copy-done.13), kind=kCustom, calls=%fused_computation | custom fusion | bytes 29360184 | tf_op jit(solution)/shard_map/gather | solution.py:85
  69.6 39.1 %all-gather.1 = f32[16,1,14]{2,1,0:T(1,128)S(1)} all-gather(f32[1,1,14]{2,1,0:T(1,128)S(1)} %bitcast.114), channel_id=1, replica_groups=mesh['req'=16,'mlp'=8] {'req'}, dimensions={0}, use_global_device_ids=true | all-gather | bytes 952 | tf_op jit(solution)/shard_map/all_gather | solution.py:26
  113.6 4.1 fusion.58
  117.7 6.2 %fusion.30 = bf16[2,224,512]{2,1,0:T(8,128)(2,1)} fusion(bf16[1536,2,224]{0,2,1:T(8,128)(2,1)} %bitcast.105, f32[2,512]{1,0:T(2,128)S(1)} %fusion.58, pred[512,1536]{0,1:T(8,128)(4,1)} %compare_and_fusion, bf16[1536,2,224]{0,2,1:T(8,128)(2,1)} %bitcast.104, bf16[512,2,224]{0,2,1:T(8,128)(2,1)} %bitcast.116), kind=kOutput, calls=%fused_computation.49 | convolution fusion | flops 1417382400 | bytes 4460544 | tf_op jit(solution)/shard_map/while/body/eval_jaxpr/hqk,khd->qhd/dot_general | solution.py:55
  123.9 43.8 %while.18 = (s32[]{:T(128)}, f32[14,64,64]{2,1,0:T(8,128)}, s32[]{:T(128)}, f32[16,14]{1,0:T(8,128)S(1)}, f32[16,14,64,64]{3,2,1,0:T(8,128)}, /*index=5*/s32[]{:T(128)}, s32[]{:T(128)}) while((s32[]{:T(128)}, f32[14,64,64]{2,1,0:T(8,128)}, s32[]{:T(128)}, f32[16,14]{1,0:T(8,128)S(1)}, f32[16,14,64,64]{3,2,1,0:T(8,128)}, ...), condition=%wide.region_5.6_spmd.clone, body=%wide.region_4.5_spmd.clone.sunk | while | flops 229380 | bytes 688401 | solution.py:36
  170.0 20.4 %fusion.21 = f32[512,14,64]{0,2,1:T(8,128)} fusion(f32[14,512,64]{1,2,0:T(8,128)S(1)} %fusion.37, f32[512,14,64]{0,2,1:T(8,128)S(1)} %bitcast.98, f32[14,512,512]{2,1,0:T(8,128)} %gather_fusion, f32[14,512]{1,0:T(8,128)S(1)} %bitcast.111, pred[512,512]{1,0:T(8,128)(4,1)S(1)} %copy-done.9, f32[14]{0:T(128)S(1)} %copy-done.18, f32[512,14]{0,1:T(8,128)S(1)} %copy-done.12, ...), kind=kOutput, calls=%fused_computation.38 | convolution fusion | flops 2831876096 | bytes 20533304 | tf_op jit(solution)/shard_map/htu,uhp->thp/dot_general | solution.py:84
  190.5 2.8 copy.80
  193.2 3.4 fusion.56
  196.7 2.8 copy.81
  201.1 12.4 %psum.21 = f32[512,2]{0,1:T(2,128)S(1)} all-reduce(f32[512,2]{0,1:T(2,128)S(1)} %reduce_sum.38), channel_id=1, replica_groups=mesh['req'=16,'mlp'=8] {'mlp'}, use_global_device_ids=true, to_apply=%region_7.8 | all-reduce | flops 1024 | bytes 8192 | tf_op jit(solution)/shard_map/psum | solution.py:235
  215.0 2.7 copy.82
  217.8 8.2 %fusion.35 = f32[512,3584]{1,0:T(8,128)S(1)} fusion(bf16[896,3584]{1,0:T(8,128)(2,1)} %param.38, f32[512,896]{1,0:T(8,128)} %copy.82, f32[896]{0:T(1024)S(1)} %copy-done.17, f32[512,896]{1,0:T(8,128)} %copy.80, bf16[512,896]{1,0:T(8,128)(2,1)} %param.30), kind=kOutput, calls=%fused_computation.57 | convolution fusion | flops 3292463104 | bytes 18353664 | tf_op jit(solution)/shard_map/dot_general | solution.py:243
  228.2 3.0 copy-done.2
  231.5 5.8 dynamic_update_slice.6
  239.3 88.7 %all-reduce.2.cloned.1.call-done = f32[512,3584]{1,0:T(8,128)} async-done(((f32[512,3584]{1,0:T(8,128)}), f32[512,3584]{1,0:T(8,128)}) %all-reduce.2.cloned.1.call-update) | async-done | bytes 7340048 | tf_op jit(solution)/shard_map/psum | solution.py:251
  328.1 3.6 multiply_reduce_fusion
  331.7 60.3 %all-gather.7.cloned.1.call-done = bf16[3584,896]{1,0:T(8,128)(2,1)} async-done(((bf16[224,896]{1,0:T(8,128)(2,1)}), bf16[3584,896]{1,0:T(8,128)(2,1)}) %all-gather.7.cloned.1.call-update) | async-done | bytes 6422544 | tf_op jit(solution)/shard_map/all_gather | solution.py:257
  392.0 8.4 %fusion.57 = f32[512,896]{1,0:T(8,128)S(1)} fusion(bf16[3584,896]{1,0:T(8,128)(2,1)} %all-gather.7.cloned.1.call-done, f32[512,3584]{1,0:T(8,128)} %all-reduce.2.cloned.1.call-done, f32[3584]{0:T(1024)S(1)} %copy-done.16, f32[512]{0:T(512)S(1)} %add_rsqrt_fusion.2), kind=kOutput, calls=%fused_computation.98 | convolution fusion | flops 3293839360 | bytes 15613952 | tf_op jit(solution)/shard_map/dot_general | solution.py:255
  400.5 55.1 %all-gather.11.cloned.1.call-done = bf16[896,3584]{0,1:T(8,128)(2,1)} async-done(((bf16[896,224]{0,1:T(8,128)(2,1)}), bf16[896,3584]{0,1:T(8,128)(2,1)}) %all-gather.11.cloned.1.call-update) | async-done | bytes 6422544 | tf_op jit(solution)/shard_map/all_gather | solution.py:268
  455.6 63.6 %all-gather.9.cloned.1.call-done = bf16[3584,896]{1,0:T(8,128)(2,1)} async-done(((bf16[224,896]{1,0:T(8,128)(2,1)}), bf16[3584,896]{1,0:T(8,128)(2,1)}) %all-gather.9.cloned.1.call-update) | async-done | bytes 6422544 | tf_op jit(solution)/shard_map/all_gather | solution.py:262
  519.2 17.7 %convolution_bitcast_fusion = f32[3584,512]{1,0:T(8,128)} fusion(bf16[896,3584]{0,1:T(8,128)(2,1)} %all-gather.11.cloned.1.call-done, f32[512,896]{1,0:T(8,128)S(1)} %fusion.57, bf16[3584,896]{1,0:T(8,128)(2,1)} %all-gather.9.cloned.1.call-done, f32[512,3584]{1,0:T(8,128)} %all-reduce.2.cloned.1.call-done, f32[3584]{0:T(1024)S(1)} %copy-done.16, ...), kind=kOutput, calls=%fused_computation.19 | convolution fusion | flops 6584926208 | bytes 29376512
  546.0 38.0 %reduce-scatter.4.cloned.1.call-done = f32[448,512]{1,0:T(8,128)} async-done(((f32[3584,512]{1,0:T(8,128)}), f32[448,512]{1,0:T(8,128)}) %reduce-scatter.4.cloned.1.call-update) | async-done | bytes 917520
  584.1 2.7 copy.96
  586.7 2.8 fusion.31
  589.6 13.2 %psum.23 = f32[512]{0:T(512)S(1)} all-reduce(f32[512]{0:T(512)S(1)} %get-tuple-element.167), channel_id=1, replica_groups=mesh['req'=16,'mlp'=8] {'mlp'}, use_global_device_ids=true, to_apply=%region_12.13 | all-reduce | flops 512 | bytes 4096 | tf_op jit(solution)/shard_map/psum | solution.py:274
  (151 shorter events, 86.1 us)
Async XLA Ops:
  7.2 218.8 %copy-start = (bf16[448,3584]{1,0:T(8,128)(2,1)S(1)}, bf16[448,3584]{1,0:T(8,128)(2,1)}, u32[]{:S(2)}) copy-start(bf16[448,3584]{1,0:T(8,128)(2,1)} %param.37) | copy-start | bytes 9633796
  7.2 116.7 %all-gather.13.cloned.1.call-start = ((), (), s32[]{:S(2)}) async-start(), calls=%async_computation.5 | async-start | bytes 7798784 | tf_op jit(solution)/shard_map/all_gather | solution.py:26
  8.7 12.3 %collective-permute-start.3 = (s32[512]{0:T(512)}, s32[512]{0:T(512)S(1)}, u32[]{:S(2)}, u32[]{:S(2)}) collective-permute-start(s32[512]{0:T(512)} %broadcast_add_fusion.3), channel_id=1, source_target_pairs={{0,8},{8,16},{16,24},{24,32},{32,40},{40,48},{48,56},{56,64},{64,7... | collective-permute-start | bytes 6152 | tf_op jit(solution)/shard_map/ppermute | solution.py:21
  14.5 6.4 %copy-start.13 = (s32[1024]{0:T(1024)}, s32[1024]{0:T(1024)S(1)}, u32[]{:S(2)}) copy-start(s32[1024]{0:T(1024)S(1)} %pad_clamp_fusion) | copy-start | bytes 12292
  19.4 3.4 copy-start.11
  19.4 6.2 copy-start.10
  29.1 298.9 %all-reduce.2.cloned.1.call-start = ((), (), s32[]{:S(2)}) async-start(), calls=%async_computation.1 | async-start | bytes 14680064 | tf_op jit(solution)/shard_map/psum | solution.py:251
  29.2 37.8 %collective-permute-start.2 = (s32[512]{0:T(512)}, s32[512]{0:T(512)}, u32[]{:S(2)}, u32[]{:S(2)}) collective-permute-start(s32[512]{0:T(512)} %broadcast_add_fusion.3), channel_id=1, source_target_pairs={{0,16},{8,24},{16,32},{24,40},{32,48},{40,56},{48,64},{56,72},{64,... | collective-permute-start | bytes 6152 | tf_op jit(solution)/shard_map/ppermute | solution.py:21
  34.6 74.2 %collective-permute-start.4 = (bf16[512,448]{0,1:T(8,128)(2,1)}, bf16[512,448]{0,1:T(8,128)(2,1)}, u32[]{:S(2)}, u32[]{:S(2)}) collective-permute-start(bf16[512,448]{0,1:T(8,128)(2,1)} %param.25), channel_id=1, source_target_pairs={{0,16},{8,24},{16,32},{24,40},{32,48},{40,56},{48,64},{56,72},{64,... | collective-permute-start | bytes 1376264 | tf_op jit(solution)/shard_map/ppermute | solution.py:21
  38.7 70.1 %collective-permute-start.5 = (bf16[512,448]{0,1:T(8,128)(2,1)}, bf16[512,448]{0,1:T(8,128)(2,1)}, u32[]{:S(2)}, u32[]{:S(2)}) collective-permute-start(bf16[512,448]{0,1:T(8,128)(2,1)} %param.25), channel_id=1, source_target_pairs={{0,8},{8,16},{16,24},{24,32},{32,40},{40,48},{48,56},{56,64},{64,7... | collective-permute-start | bytes 1376264 | tf_op jit(solution)/shard_map/ppermute | solution.py:21
  43.0 68.3 %collective-permute-start = (bf16[512,448]{0,1:T(8,128)(2,1)}, bf16[512,448]{0,1:T(8,128)(2,1)}, u32[]{:S(2)}, u32[]{:S(2)}) collective-permute-start(bf16[512,448]{0,1:T(8,128)(2,1)} %param.26), channel_id=1, source_target_pairs={{0,16},{8,24},{16,32},{24,40},{32,48},{40,56},{48,64},{56,72},{64,... | collective-permute-start | bytes 1376264 | tf_op jit(solution)/shard_map/ppermute | solution.py:21
  47.0 64.3 %collective-permute-start.1 = (bf16[512,448]{0,1:T(8,128)(2,1)}, bf16[512,448]{0,1:T(8,128)(2,1)}, u32[]{:S(2)}, u32[]{:S(2)}) collective-permute-start(bf16[512,448]{0,1:T(8,128)(2,1)} %param.26), channel_id=1, source_target_pairs={{0,8},{8,16},{16,24},{24,32},{32,40},{40,48},{48,56},{56,64},{64,7... | collective-permute-start | bytes 1376264 | tf_op jit(solution)/shard_map/ppermute | solution.py:21
  56.1 13.5 %copy-start.15 = (f32[14]{0:T(128)S(1)}, f32[14]{0:T(128)}, u32[]{:S(2)}) copy-start(f32[14]{0:T(128)} %get-tuple-element.156) | copy-start | bytes 172
  66.9 44.3 %copy-start.6 = (bf16[512,448]{0,1:T(8,128)(2,1)S(1)}, bf16[512,448]{0,1:T(8,128)(2,1)}, u32[]{:S(2)}) copy-start(bf16[512,448]{0,1:T(8,128)(2,1)} %param.26) | copy-start | bytes 1376260
  167.6 2.3 copy-start.3
  167.6 2.3 copy-start.9
  167.6 2.4 copy-start.12
  167.6 2.4 copy-start.18
  213.5 4.2 copy-start.17
  217.8 8.2 %copy-start.8 = (bf16[2,224,512]{2,1,0:T(8,128)(2,1)S(1)}, bf16[2,224,512]{2,1,0:T(8,128)(2,1)}, u32[]{:S(2)}) copy-start(bf16[2,224,512]{2,1,0:T(8,128)(2,1)} %fusion.30) | copy-start | bytes 1376260
  226.0 5.2 copy-start.4
  228.2 3.0 copy-start.2
  237.4 154.6 %all-gather.7.cloned.1.call-start = ((), (), s32[]{:S(2)}) async-start(), calls=%async_computation.2 | async-start | bytes 6823936 | tf_op jit(solution)/shard_map/all_gather | solution.py:257
  238.1 217.5 %all-gather.11.cloned.1.call-start = ((), (), s32[]{:S(2)}) async-start(), calls=%async_computation.4 | async-start | bytes 6823936 | tf_op jit(solution)/shard_map/all_gather | solution.py:268
  238.7 280.5 %all-gather.9.cloned.1.call-start = ((), (), s32[]{:S(2)}) async-start(), calls=%async_computation.3 | async-start | bytes 6823936 | tf_op jit(solution)/shard_map/all_gather | solution.py:262
  239.3 152.7 %copy-start.16 = (f32[3584]{0:T(1024)S(1)}, f32[3584]{0:T(1024)}, u32[]{:S(2)}) copy-start(f32[3584]{0:T(1024)} %param.39) | copy-start | bytes 43012
  239.3 344.8 %reduce-scatter.4.cloned.1.call-start = ((), (), s32[]{:S(2)}) async-start(), calls=%async_computation.6 | async-start | bytes 8257536
  536.9 1.0 copy-start.5
  536.9 1.2 copy-start.7
  540.0 2.0 copy-start.19
  584.1 20.8 %copy-start.14 = (f32[448]{0:T(512)S(1)}, f32[448]{0:T(512)}, u32[]{:S(2)}) copy-start(f32[448]{0:T(512)} %param.43) | copy-start | bytes 5380
  584.1 24.8 %copy-start.1 = (bf16[448,3584]{1,0:T(8,128)(2,1)S(1)}, bf16[448,3584]{1,0:T(8,128)(2,1)}, u32[]{:S(2)}) copy-start(bf16[448,3584]{1,0:T(8,128)(2,1)} %param.37) | copy-start | bytes 9633796
Sparse Core Ops, SparseCore 0:
  29.2 88.2 all-gather.12
  237.5 90.5 all-reduce.1
  330.2 61.7 all-gather.6
  394.0 61.5 all-gather.10
  457.6 61.5 all-gather.8
  537.1 46.9 reduce-scatter.3
where the time goes:
time: 626 us; the launch traced here: 616 us
  waiting for transfers between devices  308 us (49%)
  matrix products  75 us (12%)
  blocking collectives  64.8 us (10%)
  other arithmetic  61.3 us (10%)
  local copies, waits for them, and re-layouts  55 us (9%)
  starting transfers between devices  25.2 us (4%)
  between operations  16.2 us (3%)
  loops' own time  11.1 us (2%)
    psum x1, waiting for transfers between devices, body(): lax.psum(lax.dynamic_update_slice_in_dim(projected, own_part, offset, 1),...  88.7 us
    all_gather x1, waiting for transfers between devices, body(): lax.all_gather(up_proj, 'req', axis=0, tiled=True)  63.6 us
    all_gather x1, waiting for transfers between devices, body(): lax.all_gather(gate_proj, 'req', axis=0, tiled=True)  60.3 us
    all_gather x1, waiting for transfers between devices, body(): lax.all_gather(down_proj, 'req', axis=1, tiled=True)  55.1 us
    unnamed x7, waiting for transfers between devices  39.8 us
    all_gather x1, blocking collectives, entering(): everything = jax.tree.map(lambda part: lax.all_gather(part, axis), x)  39.1 us
    select_n x16, other arithmetic, step(): return jax.tree.map(lambda a, b: jnp.where(reached, a, b), new, before)  32.6 us
    ppermute x6, starting transfers between devices, from_behind(): lax.ppermute(value, axis, [(source, source + steps) for source in range(l...  25 us
  transfers between devices with their start and end apart: 12, of which 5 were waited for; matrix products, arithmetic and copies ran while one was open for 10% of the time, Pallas kernels for 0%

commit v1 on v0

--- a/solution.py
+++ b/solution.py
@@ -13,6 +13,20 @@
 PAGE = 16
 EPSILON = 1e-05
 exact_mode = lax.Precision.HIGHEST
+
+
+def feed_rounds(mine_x, in_dim=0):
+    lanes = lax.axis_size("req")
+    rack = [(q, (q + 1) % lanes) for q in range(lanes)]
+    store = [(q, (q - 1) % lanes) for q in range(lanes)]
+    current_block, val2 = ([mine_x], [mine_x])
+    for _ in range(lanes // 2):
+        current_block.append(lax.ppermute(current_block[-1], "req", rack))
+    for _ in [*range((lanes - 1) // 2)]:
+        after = lax.ppermute(val2[-1], "req", store)
+        val2.append(after)
+    o_now = jnp.concatenate([*current_block[::-1], *val2[1:]], in_dim)
+    return jnp.roll(o_now, (lax.axis_index("req") - lanes // 2) * mine_x.shape[in_dim], in_dim)
 
 
 def from_behind(value, axis, steps):
@@ -257,11 +271,7 @@
         lax.all_gather(gate_proj, "req", axis=0, tiled=True),
         preferred_element_type=jnp.float32,
     )
-    up_act = jnp.dot(
-        normed,
-        lax.all_gather(up_proj, "req", axis=0, tiled=True),
-        preferred_element_type=jnp.float32,
-    )
+    up_act = jnp.dot(normed, feed_rounds(up_proj), preferred_element_type=jnp.float32)
     latent_activation = (jax.nn.silu(gate_act) * up_act).astype(jnp.bfloat16)
     partial_value = jnp.dot(
         latent_activation,

time: 626 us -> 544 us (0.87)
  waiting for transfers between devices: 308 us -> 148 us
  local copies, waits for them, and re-layouts: 55 us -> 101 us
  starting transfers between devices: 25.2 us -> 65.5 us
  loops' own time: 11.1 us -> 0.5 us
    psum x1, waiting for transfers between devices: 88.7 us -> 0.01 us  [body(): lax.psum(lax.dynamic_update_slice_in_dim(projected, own_part, offset, 1),...]
    all_gather x1 -> x0, waiting for transfers between devices: 63.6 us -> none  [body(): lax.all_gather(up_proj, 'req', axis=0, tiled=True)]
    ppermute x0 -> x15, waiting for transfers between devices: none -> 59.1 us  [the longest x8 57.9 us: feed_rounds(): current_block.append(lax.ppermute(current_block[-1], 'req', rack))]
    all_gather x1, waiting for transfers between devices: 60.3 us -> 12.8 us  [body(): lax.all_gather(gate_proj, 'req', axis=0, tiled=True)]
    ppermute x0 -> x15, starting transfers between devices: none -> 40.2 us  [the longest x7 38.4 us: feed_rounds(): after = lax.ppermute(val2[-1], 'req', store)]
    unnamed x51 -> x94, local copies, waits for them, and re-layouts: 16.2 us -> 54 us
    another operation x1, loops' own time: 11.1 us -> 0.5 us  [entering(): return lax.fori_loop(0, devices, step, start)]
    all_gather x1, waiting for transfers between devices: 55.1 us -> 45.6 us  [body(): lax.all_gather(down_proj, 'req', axis=1, tiled=True)]
  transfers between devices with their start and end apart: 12 -> 26, of which waited for: 5 -> 13; matrix products, arithmetic and copies ran while one was open for 10% -> 22% of each run, Pallas kernels for 0% -> 0%
where the time goes in v1:
time: 544 us; the launch traced here: 534 us
  waiting for transfers between devices  148 us (27%)
  local copies, waits for them, and re-layouts  101 us (19%)
  matrix products  76.2 us (14%)
  starting transfers between devices  65.5 us (12%)
  blocking collectives  65 us (12%)
  other arithmetic  61.6 us (11%)
  between operations  15.8 us (3%)
    ppermute x8, waiting for transfers between devices, feed_rounds(): current_block.append(lax.ppermute(current_block[-1], 'req', rack))  57.9 us
    unnamed x94, local copies, waits for them, and re-layouts  54 us
    all_gather x1, waiting for transfers between devices, body(): lax.all_gather(down_proj, 'req', axis=1, tiled=True)  45.6 us
    all_gather x1, blocking collectives, entering(): everything = jax.tree.map(lambda part: lax.all_gather(part, axis), x)  39.3 us
    ppermute x7, starting transfers between devices, feed_rounds(): after = lax.ppermute(val2[-1], 'req', store)  38.4 us
    select_n x16, other arithmetic, step(): return jax.tree.map(lambda a, b: jnp.where(reached, a, b), new, before)  32.6 us
    unnamed x6, waiting for transfers between devices  30.3 us
    ppermute x6, starting transfers between devices, from_behind(): lax.ppermute(value, axis, [(source, source + steps) for source in range(l...  25.1 us
  transfers between devices with their start and end apart: 26, of which 13 were waited for; matrix products, arithmetic and copies ran while one was open for 22% of the time, Pallas kernels for 0%

profile of v1, /device:TPU:0, one launch (start us, length us, event | category | flops | bytes accessed | tf_op | source)
XLA Modules:
  0.0 533.8 jit_solution(1826448649908160974)
XLA Ops:
  29.2 5.3 %collective-permute-start.2 = (s32[512]{0:T(512)}, s32[512]{0:T(512)}, u32[]{:S(2)}, u32[]{:S(2)}) collective-permute-start(s32[512]{0:T(512)} %broadcast_add_fusion.3), channel_id=1, source_target_pairs={{0,16},{8,24},{16,32},{24,40},{32,48},{40,56},{48,64},{56,72},{64,... | collective-permute-start | bytes 6152 | tf_op jit(solution)/shard_map/ppermute | solution.py:35
  56.1 8.7 %gather_fusion = f32[14,512,512]{2,1,0:T(8,128)} fusion(f32[2,512,512]{2,1,0:T(8,128)} %fusion.63, s32[1024]{0:T(1024)} %copy-done.19), kind=kCustom, calls=%fused_computation | custom fusion | bytes 29360184 | tf_op jit(solution)/shard_map/gather | solution.py:99
  69.4 39.3 %all-gather.1 = f32[16,1,14]{2,1,0:T(1,128)S(1)} all-gather(f32[1,1,14]{2,1,0:T(1,128)S(1)} %bitcast.114), channel_id=1, replica_groups=mesh['req'=16,'mlp'=8] {'req'}, dimensions={0}, use_global_device_ids=true | all-gather | bytes 952 | tf_op jit(solution)/shard_map/all_gather | solution.py:40
  117.9 6.2 %fusion.34 = bf16[2,224,512]{2,1,0:T(8,128)(2,1)} fusion(bf16[1536,2,224]{0,2,1:T(8,128)(2,1)} %bitcast.105, f32[2,512]{1,0:T(2,128)S(1)} %fusion.62, pred[512,1536]{0,1:T(8,128)(4,1)} %compare_and_fusion, bf16[1536,2,224]{0,2,1:T(8,128)(2,1)} %bitcast.104, bf16[512,2,224]{0,2,1:T(8,128)(2,1)} %bitcast.116), kind=kOutput, calls=%fused_computation.51 | convolution fusion | flops 1417382400 | bytes 4460544 | tf_op jit(solution)/shard_map/while/body/eval_jaxpr/hqk,khd->qhd/dot_general | solution.py:69
  124.1 33.2 %while.18 = (s32[]{:T(128)}, f32[14,64,64]{2,1,0:T(8,128)}, s32[]{:T(128)}, f32[16,14]{1,0:T(8,128)S(1)}, f32[16,14,64,64]{3,2,1,0:T(8,128)}, /*index=5*/s32[]{:T(128)}, s32[]{:T(128)}) while((s32[]{:T(128)}, f32[14,64,64]{2,1,0:T(8,128)}, s32[]{:T(128)}, f32[16,14]{1,0:T(8,128)S(1)}, f32[16,14,64,64]{3,2,1,0:T(8,128)}, ...), condition=%wide.region_5.6_spmd.clone, body=%wide.region_4.5_spmd.clone.sunk | while | flops 229380 | bytes 688401 | solution.py:50
  159.5 21.0 %fusion.23 = f32[512,14,64]{0,2,1:T(8,128)} fusion(f32[14,512,64]{1,2,0:T(8,128)S(1)} %fusion.41, f32[512,14,64]{0,2,1:T(8,128)} %bitcast.98, f32[14,512,512]{2,1,0:T(8,128)} %gather_fusion, f32[14,512]{1,0:T(8,128)S(1)} %bitcast.111, pred[512,512]{1,0:T(8,128)(4,1)S(1)} %copy-done.16, f32[14]{0:T(128)S(1)} %copy-done.24, ...), kind=kOutput, calls=%fused_computation.40 | convolution fusion | flops 2831876096 | bytes 20533304 | tf_op jit(solution)/shard_map/htu,uhp->thp/dot_general | solution.py:98
  191.2 12.4 %psum.21 = f32[512,2]{0,1:T(2,128)S(1)} all-reduce(f32[512,2]{0,1:T(2,128)S(1)} %reduce_sum.38), channel_id=1, replica_groups=mesh['req'=16,'mlp'=8] {'mlp'}, use_global_device_ids=true, to_apply=%region_7.8 | all-reduce | flops 1024 | bytes 8192 | tf_op jit(solution)/shard_map/psum | solution.py:249
  208.1 8.2 %fusion.39 = f32[512,3584]{1,0:T(8,128)S(1)} fusion(bf16[896,3584]{1,0:T(8,128)(2,1)} %param.38, f32[512,896]{1,0:T(8,128)} %copy.82, f32[896]{0:T(1024)S(1)} %copy-done.23, f32[512,896]{1,0:T(8,128)} %copy.80, bf16[512,896]{1,0:T(8,128)(2,1)} %param.30), kind=kOutput, calls=%fused_computation.59 | convolution fusion | flops 3292463104 | bytes 18353664 | tf_op jit(solution)/shard_map/dot_general | solution.py:257
  221.9 5.8 %dynamic_update_slice.6 = f32[512,3584]{1,0:T(8,128)} dynamic-update-slice(f32[512,3584]{1,0:T(8,128)} %copy-done.2, f32[512,448]{1,0:T(8,128)S(1)} %convert_add_fusion, s32[]{:T(128)} %constant.119.clone.1, s32[]{:T(128)S(6)} %select_n.116) | dynamic-update-slice | bytes 1835012 | tf_op jit(solution)/shard_map/dynamic_update_slice | solution.py:265
  230.9 13.2 %collective-permute-done.6 = bf16[224,896]{1,0:T(8,128)(2,1)S(1)} collective-permute-done((bf16[224,896]{1,0:T(8,128)(2,1)S(1)}, bf16[224,896]{1,0:T(8,128)(2,1)S(1)}, u32[]{:S(2)}, u32[]{:S(2)}) %collective-permute-start.6) | collective-permute-done | bytes 401440 | tf_op jit(solution)/shard_map/ppermute | solution.py:24
  244.1 5.3 %collective-permute-start.14 = (bf16[224,896]{1,0:T(8,128)(2,1)S(1)}, bf16[224,896]{1,0:T(8,128)(2,1)S(1)}, u32[]{:S(2)}, u32[]{:S(2)}) collective-permute-start(bf16[224,896]{1,0:T(8,128)(2,1)S(1)} %copy-done.6), channel_id=1, source_target_pairs={{0,120},{8,0},{16,8},{24,16},{32,24},{40,32},{48,40},{56,48},{64,5... | collective-permute-start | bytes 1204232 | tf_op jit(solution)/shard_map/ppermute | solution.py:26
  249.5 8.8 %collective-permute-done.7 = bf16[224,896]{1,0:T(8,128)(2,1)S(1)} collective-permute-done((bf16[224,896]{1,0:T(8,128)(2,1)S(1)}, bf16[224,896]{1,0:T(8,128)(2,1)S(1)}, u32[]{:S(2)}, u32[]{:S(2)}) %collective-permute-start.7) | collective-permute-done | bytes 401440 | tf_op jit(solution)/shard_map/ppermute | solution.py:24
  258.3 5.3 %collective-permute-start.15 = (bf16[224,896]{1,0:T(8,128)(2,1)S(1)}, bf16[224,896]{1,0:T(8,128)(2,1)S(1)}, u32[]{:S(2)}, u32[]{:S(2)}) collective-permute-start(bf16[224,896]{1,0:T(8,128)(2,1)S(1)} %collective-permute-done.14), channel_id=1, source_target_pairs={{0,120},{8,0},{16,8},{24,16},{32,24},{40,32},{48,40},{56,48},{64,5... | collective-permute-start | bytes 1204232 | tf_op jit(solution)/shard_map/ppermute | solution.py:26
  263.6 7.9 %collective-permute-done.8 = bf16[224,896]{1,0:T(8,128)(2,1)S(1)} collective-permute-done((bf16[224,896]{1,0:T(8,128)(2,1)S(1)}, bf16[224,896]{1,0:T(8,128)(2,1)S(1)}, u32[]{:S(2)}, u32[]{:S(2)}) %collective-permute-start.8) | collective-permute-done | bytes 401440 | tf_op jit(solution)/shard_map/ppermute | solution.py:24
  271.5 5.3 %collective-permute-start.16 = (bf16[224,896]{1,0:T(8,128)(2,1)S(1)}, bf16[224,896]{1,0:T(8,128)(2,1)S(1)}, u32[]{:S(2)}, u32[]{:S(2)}) collective-permute-start(bf16[224,896]{1,0:T(8,128)(2,1)S(1)} %collective-permute-done.15), channel_id=1, source_target_pairs={{0,120},{8,0},{16,8},{24,16},{32,24},{40,32},{48,40},{56,48},{64,5... | collective-permute-start | bytes 1204232 | tf_op jit(solution)/shard_map/ppermute | solution.py:26
  276.9 7.0 %collective-permute-done.9 = bf16[224,896]{1,0:T(8,128)(2,1)S(1)} collective-permute-done((bf16[224,896]{1,0:T(8,128)(2,1)S(1)}, bf16[224,896]{1,0:T(8,128)(2,1)S(1)}, u32[]{:S(2)}, u32[]{:S(2)}) %collective-permute-start.9) | collective-permute-done | bytes 401440 | tf_op jit(solution)/shard_map/ppermute | solution.py:24
  283.9 5.3 %collective-permute-start.17 = (bf16[224,896]{1,0:T(8,128)(2,1)S(1)}, bf16[224,896]{1,0:T(8,128)(2,1)S(1)}, u32[]{:S(2)}, u32[]{:S(2)}) collective-permute-start(bf16[224,896]{1,0:T(8,128)(2,1)S(1)} %collective-permute-done.16), channel_id=1, source_target_pairs={{0,120},{8,0},{16,8},{24,16},{32,24},{40,32},{48,40},{56,48},{64,5... | collective-permute-start | bytes 1204232 | tf_op jit(solution)/shard_map/ppermute | solution.py:26
  289.2 6.1 %collective-permute-done.10 = bf16[224,896]{1,0:T(8,128)(2,1)S(1)} collective-permute-done((bf16[224,896]{1,0:T(8,128)(2,1)S(1)}, bf16[224,896]{1,0:T(8,128)(2,1)S(1)}, u32[]{:S(2)}, u32[]{:S(2)}) %collective-permute-start.10) | collective-permute-done | bytes 401440 | tf_op jit(solution)/shard_map/ppermute | solution.py:24
  296.1 5.3 collective-permute-start.18
  301.4 5.1 collective-permute-done.11
  306.8 5.9 %collective-permute-start.19 = (bf16[224,896]{1,0:T(8,128)(2,1)}, bf16[224,896]{1,0:T(8,128)(2,1)}, u32[]{:S(2)}, u32[]{:S(2)}) collective-permute-start(bf16[224,896]{1,0:T(8,128)(2,1)} %collective-permute-done.18), channel_id=1, source_target_pairs={{0,120},{8,0},{16,8},{24,16},{32,24},{40,32},{48,40},{56,48},{64,5... | collective-permute-start | bytes 1204232 | tf_op jit(solution)/shard_map/ppermute | solution.py:26
  312.7 5.1 collective-permute-done.12
  318.7 5.8 %collective-permute-start.20 = (bf16[224,896]{1,0:T(8,128)(2,1)}, bf16[224,896]{1,0:T(8,128)(2,1)S(1)}, u32[]{:S(2)}, u32[]{:S(2)}) collective-permute-start(bf16[224,896]{1,0:T(8,128)(2,1)} %collective-permute-done.19), channel_id=1, source_target_pairs={{0,120},{8,0},{16,8},{24,16},{32,24},{40,32},{48,40},{56,48},{64,5... | collective-permute-start | bytes 1204232 | tf_op jit(solution)/shard_map/ppermute | solution.py:26
  324.5 4.8 collective-permute-done.13
  369.8 12.8 %all-gather.6.cloned.1.call-done = bf16[3584,896]{1,0:T(8,128)(2,1)} async-done(((bf16[224,896]{1,0:T(8,128)(2,1)}), bf16[3584,896]{1,0:T(8,128)(2,1)}) %all-gather.6.cloned.1.call-update) | async-done | bytes 6422544 | tf_op jit(solution)/shard_map/all_gather | solution.py:271
  382.6 8.5 %fusion.61 = f32[512,896]{1,0:T(8,128)S(1)} fusion(bf16[3584,896]{1,0:T(8,128)(2,1)} %all-gather.6.cloned.1.call-done, f32[512,3584]{1,0:T(8,128)} %all-reduce.2.cloned.1.call-done, f32[3584]{0:T(1024)S(1)} %copy-done.22, f32[512]{0:T(512)S(1)} %add_rsqrt_fusion.2), kind=kOutput, calls=%fused_computation.132 | convolution fusion | flops 3293839360 | bytes 15613952 | tf_op jit(solution)/shard_map/dot_general | solution.py:269
  391.0 9.5 %multiply_convert_fusion.1 = bf16[512,896]{1,0:T(8,128)(2,1)S(1)} fusion(f32[512,896]{1,0:T(8,128)S(1)} %fusion.61, bf16[7168,896]{1,0:T(8,128)(2,1)} %constant_dynamic-update-slice_fusion, s32[]{:T(128)S(6)} %select_n.118, f32[512,3584]{1,0:T(8,128)} %all-reduce.2.cloned.1.call-done, f32[3584]{0:T(1024)S(1)} %copy-done.22, f32[512]{0:T(512)S(1)} %add_rsqrt_fusion.2), kind=kOutput, calls=%fused_computation.41 | convolution fusion | flops 3296591872 | bytes 16531460 | tf_op jit(solution)/shard_map/dot_general | solution.py:274
  400.6 45.6 %all-gather.8.cloned.1.call-done = bf16[896,3584]{0,1:T(8,128)(2,1)} async-done(((bf16[896,224]{0,1:T(8,128)(2,1)}), bf16[896,3584]{0,1:T(8,128)(2,1)}) %all-gather.8.cloned.1.call-update) | async-done | bytes 6422544 | tf_op jit(solution)/shard_map/all_gather | solution.py:278
  446.1 8.9 %convolution_bitcast_fusion = f32[3584,512]{1,0:T(8,128)} fusion(bf16[512,896]{1,0:T(8,128)(2,1)S(1)} %multiply_convert_fusion.1, bf16[896,3584]{0,1:T(8,128)(2,1)} %all-gather.8.cloned.1.call-done), kind=kOutput, calls=%fused_computation.19 | convolution fusion | flops 3288334336 | bytes 14680064
  462.4 8.5 %scatter_fusion = bf16[2,2,32,3584]{3,1,2,0:T(2,128)(2,1)} fusion(bf16[2,2,32,3584]{3,1,2,0:T(2,128)(2,1)} %broadcast_in_dim.106, s32[32]{0:T(128)S(1)} %fusion.51, bf16[32,2,2,3584]{3,2,1,0:T(2,128)(2,1)} %copy.89), kind=kCustom, calls=%fused_computation.3 | custom fusion | bytes 2752640 | tf_op jit(solution)/shard_map/scatter | solution.py:211
  473.2 29.0 %reduce-scatter.4.cloned.1.call-done = f32[448,512]{1,0:T(8,128)} async-done(((f32[3584,512]{1,0:T(8,128)}), f32[448,512]{1,0:T(8,128)}) %reduce-scatter.4.cloned.1.call-update) | async-done | bytes 917520
  507.6 13.2 %psum.23 = f32[512]{0:T(512)S(1)} all-reduce(f32[512]{0:T(512)S(1)} %get-tuple-element.167), channel_id=1, replica_groups=mesh['req'=16,'mlp'=8] {'mlp'}, use_global_device_ids=true, to_apply=%region_12.13 | all-reduce | flops 512 | bytes 4096 | tf_op jit(solution)/shard_map/psum | solution.py:284
  (223 shorter events, 178.0 us)
Async XLA Ops:
  7.2 209.1 %copy-start = (bf16[448,3584]{1,0:T(8,128)(2,1)S(1)}, bf16[448,3584]{1,0:T(8,128)(2,1)}, u32[]{:S(2)}) copy-start(bf16[448,3584]{1,0:T(8,128)(2,1)} %param.37) | copy-start | bytes 9633796
  7.2 116.9 %all-gather.10.cloned.1.call-start = ((), (), s32[]{:S(2)}) async-start(), calls=%async_computation.4 | async-start | bytes 7798784 | tf_op jit(solution)/shard_map/all_gather | solution.py:40
  8.7 12.3 %collective-permute-start.3 = (s32[512]{0:T(512)}, s32[512]{0:T(512)S(1)}, u32[]{:S(2)}, u32[]{:S(2)}) collective-permute-start(s32[512]{0:T(512)} %broadcast_add_fusion.3), channel_id=1, source_target_pairs={{0,8},{8,16},{16,24},{24,32},{32,40},{40,48},{48,56},{56,64},{64,7... | collective-permute-start | bytes 6152 | tf_op jit(solution)/shard_map/ppermute | solution.py:35
  29.1 336.8 %all-reduce.2.cloned.1.call-start = ((), (), s32[]{:S(2)}) async-start(), calls=%async_computation.1 | async-start | bytes 14680064 | tf_op jit(solution)/shard_map/psum | solution.py:265
  29.2 37.7 %collective-permute-start.2 = (s32[512]{0:T(512)}, s32[512]{0:T(512)}, u32[]{:S(2)}, u32[]{:S(2)}) collective-permute-start(s32[512]{0:T(512)} %broadcast_add_fusion.3), channel_id=1, source_target_pairs={{0,16},{8,24},{16,32},{24,40},{32,48},{40,56},{48,64},{56,72},{64,... | collective-permute-start | bytes 6152 | tf_op jit(solution)/shard_map/ppermute | solution.py:35
  34.5 74.2 %collective-permute-start.4 = (bf16[512,448]{0,1:T(8,128)(2,1)}, bf16[512,448]{0,1:T(8,128)(2,1)}, u32[]{:S(2)}, u32[]{:S(2)}) collective-permute-start(bf16[512,448]{0,1:T(8,128)(2,1)} %param.25), channel_id=1, source_target_pairs={{0,16},{8,24},{16,32},{24,40},{32,48},{40,56},{48,64},{56,72},{64,... | collective-permute-start | bytes 1376264 | tf_op jit(solution)/shard_map/ppermute | solution.py:35
  38.7 70.1 %collective-permute-start.5 = (bf16[512,448]{0,1:T(8,128)(2,1)}, bf16[512,448]{0,1:T(8,128)(2,1)}, u32[]{:S(2)}, u32[]{:S(2)}) collective-permute-start(bf16[512,448]{0,1:T(8,128)(2,1)} %param.25), channel_id=1, source_target_pairs={{0,8},{8,16},{16,24},{24,32},{32,40},{40,48},{48,56},{56,64},{64,7... | collective-permute-start | bytes 1376264 | tf_op jit(solution)/shard_map/ppermute | solution.py:35
  42.9 68.4 %collective-permute-start = (bf16[512,448]{0,1:T(8,128)(2,1)}, bf16[512,448]{0,1:T(8,128)(2,1)}, u32[]{:S(2)}, u32[]{:S(2)}) collective-permute-start(bf16[512,448]{0,1:T(8,128)(2,1)} %param.26), channel_id=1, source_target_pairs={{0,16},{8,24},{16,32},{24,40},{32,48},{40,56},{48,64},{56,72},{64,... | collective-permute-start | bytes 1376264 | tf_op jit(solution)/shard_map/ppermute | solution.py:35
  47.0 64.3 %collective-permute-start.1 = (bf16[512,448]{0,1:T(8,128)(2,1)}, bf16[512,448]{0,1:T(8,128)(2,1)}, u32[]{:S(2)}, u32[]{:S(2)}) collective-permute-start(bf16[512,448]{0,1:T(8,128)(2,1)} %param.26), channel_id=1, source_target_pairs={{0,8},{8,16},{16,24},{24,32},{32,40},{40,48},{48,56},{56,64},{64,7... | collective-permute-start | bytes 1376264 | tf_op jit(solution)/shard_map/ppermute | solution.py:35
  124.1 35.4 %copy-start.16 = (pred[512,512]{1,0:T(8,128)(4,1)S(1)}, pred[512,512]{1,0:T(8,128)(4,1)}, u32[]{:S(2)}) copy-start(pred[512,512]{1,0:T(8,128)(4,1)} %fusion.38) | copy-start | bytes 786436
  124.1 35.4 %copy-start.24 = (f32[14]{0:T(128)S(1)}, f32[14]{0:T(128)}, u32[]{:S(2)}) copy-start(f32[14]{0:T(128)} %param.35) | copy-start | bytes 172
  227.7 154.8 %all-gather.6.cloned.1.call-start = ((), (), s32[]{:S(2)}) async-start(), calls=%async_computation.2 | async-start | bytes 6823936 | tf_op jit(solution)/shard_map/all_gather | solution.py:271
  228.5 217.7 %all-gather.8.cloned.1.call-start = ((), (), s32[]{:S(2)}) async-start(), calls=%async_computation.3 | async-start | bytes 6823936 | tf_op jit(solution)/shard_map/all_gather | solution.py:278
  229.1 273.2 %reduce-scatter.4.cloned.1.call-start = ((), (), s32[]{:S(2)}) async-start(), calls=%async_computation.5 | async-start | bytes 8257536
  229.1 15.0 %collective-permute-start.6 = (bf16[224,896]{1,0:T(8,128)(2,1)S(1)}, bf16[224,896]{1,0:T(8,128)(2,1)S(1)}, u32[]{:S(2)}, u32[]{:S(2)}) collective-permute-start(bf16[224,896]{1,0:T(8,128)(2,1)S(1)} %copy-done.6), channel_id=1, source_target_pairs={{0,8},{8,16},{16,24},{24,32},{32,40},{40,48},{48,56},{56,64},{64,7... | collective-permute-start | bytes 1204232 | tf_op jit(solution)/shard_map/ppermute | solution.py:24
  244.1 14.2 %collective-permute-start.7 = (bf16[224,896]{1,0:T(8,128)(2,1)S(1)}, bf16[224,896]{1,0:T(8,128)(2,1)S(1)}, u32[]{:S(2)}, u32[]{:S(2)}) collective-permute-start(bf16[224,896]{1,0:T(8,128)(2,1)S(1)} %collective-permute-done.6), channel_id=1, source_target_pairs={{0,8},{8,16},{16,24},{24,32},{32,40},{40,48},{48,56},{56,64},{64,7... | collective-permute-start | bytes 1204232 | tf_op jit(solution)/shard_map/ppermute | solution.py:24
  244.1 14.2 %collective-permute-start.14 = (bf16[224,896]{1,0:T(8,128)(2,1)S(1)}, bf16[224,896]{1,0:T(8,128)(2,1)S(1)}, u32[]{:S(2)}, u32[]{:S(2)}) collective-permute-start(bf16[224,896]{1,0:T(8,128)(2,1)S(1)} %copy-done.6), channel_id=1, source_target_pairs={{0,120},{8,0},{16,8},{24,16},{32,24},{40,32},{48,40},{56,48},{64,5... | collective-permute-start | bytes 1204232 | tf_op jit(solution)/shard_map/ppermute | solution.py:26
  258.3 13.3 %collective-permute-start.8 = (bf16[224,896]{1,0:T(8,128)(2,1)S(1)}, bf16[224,896]{1,0:T(8,128)(2,1)S(1)}, u32[]{:S(2)}, u32[]{:S(2)}) collective-permute-start(bf16[224,896]{1,0:T(8,128)(2,1)S(1)} %collective-permute-done.7), channel_id=1, source_target_pairs={{0,8},{8,16},{16,24},{24,32},{32,40},{40,48},{48,56},{56,64},{64,7... | collective-permute-start | bytes 1204232 | tf_op jit(solution)/shard_map/ppermute | solution.py:24
  258.3 13.3 %collective-permute-start.15 = (bf16[224,896]{1,0:T(8,128)(2,1)S(1)}, bf16[224,896]{1,0:T(8,128)(2,1)S(1)}, u32[]{:S(2)}, u32[]{:S(2)}) collective-permute-start(bf16[224,896]{1,0:T(8,128)(2,1)S(1)} %collective-permute-done.14), channel_id=1, source_target_pairs={{0,120},{8,0},{16,8},{24,16},{32,24},{40,32},{48,40},{56,48},{64,5... | collective-permute-start | bytes 1204232 | tf_op jit(solution)/shard_map/ppermute | solution.py:26
  271.5 12.3 %collective-permute-start.9 = (bf16[224,896]{1,0:T(8,128)(2,1)S(1)}, bf16[224,896]{1,0:T(8,128)(2,1)S(1)}, u32[]{:S(2)}, u32[]{:S(2)}) collective-permute-start(bf16[224,896]{1,0:T(8,128)(2,1)S(1)} %collective-permute-done.8), channel_id=1, source_target_pairs={{0,8},{8,16},{16,24},{24,32},{32,40},{40,48},{48,56},{56,64},{64,7... | collective-permute-start | bytes 1204232 | tf_op jit(solution)/shard_map/ppermute | solution.py:24
  271.5 12.3 %collective-permute-start.16 = (bf16[224,896]{1,0:T(8,128)(2,1)S(1)}, bf16[224,896]{1,0:T(8,128)(2,1)S(1)}, u32[]{:S(2)}, u32[]{:S(2)}) collective-permute-start(bf16[224,896]{1,0:T(8,128)(2,1)S(1)} %collective-permute-done.15), channel_id=1, source_target_pairs={{0,120},{8,0},{16,8},{24,16},{32,24},{40,32},{48,40},{56,48},{64,5... | collective-permute-start | bytes 1204232 | tf_op jit(solution)/shard_map/ppermute | solution.py:26
  283.9 11.4 %collective-permute-start.10 = (bf16[224,896]{1,0:T(8,128)(2,1)S(1)}, bf16[224,896]{1,0:T(8,128)(2,1)S(1)}, u32[]{:S(2)}, u32[]{:S(2)}) collective-permute-start(bf16[224,896]{1,0:T(8,128)(2,1)S(1)} %collective-permute-done.9), channel_id=1, source_target_pairs={{0,8},{8,16},{16,24},{24,32},{32,40},{40,48},{48,56},{56,64},{64,7... | collective-permute-start | bytes 1204232 | tf_op jit(solution)/shard_map/ppermute | solution.py:24
  283.9 11.4 %collective-permute-start.17 = (bf16[224,896]{1,0:T(8,128)(2,1)S(1)}, bf16[224,896]{1,0:T(8,128)(2,1)S(1)}, u32[]{:S(2)}, u32[]{:S(2)}) collective-permute-start(bf16[224,896]{1,0:T(8,128)(2,1)S(1)} %collective-permute-done.16), channel_id=1, source_target_pairs={{0,120},{8,0},{16,8},{24,16},{32,24},{40,32},{48,40},{56,48},{64,5... | collective-permute-start | bytes 1204232 | tf_op jit(solution)/shard_map/ppermute | solution.py:26
  295.3 11.2 %collective-permute-start.11 = (bf16[224,896]{1,0:T(8,128)(2,1)S(1)}, bf16[224,896]{1,0:T(8,128)(2,1)S(1)}, u32[]{:S(2)}, u32[]{:S(2)}) collective-permute-start(bf16[224,896]{1,0:T(8,128)(2,1)S(1)} %collective-permute-done.10), channel_id=1, source_target_pairs={{0,8},{8,16},{16,24},{24,32},{32,40},{40,48},{48,56},{56,64},{64,7... | collective-permute-start | bytes 1204232 | tf_op jit(solution)/shard_map/ppermute | solution.py:24
  296.1 10.7 %collective-permute-start.18 = (bf16[224,896]{1,0:T(8,128)(2,1)S(1)}, bf16[224,896]{1,0:T(8,128)(2,1)}, u32[]{:S(2)}, u32[]{:S(2)}) collective-permute-start(bf16[224,896]{1,0:T(8,128)(2,1)S(1)} %collective-permute-done.17), channel_id=1, source_target_pairs={{0,120},{8,0},{16,8},{24,16},{32,24},{40,32},{48,40},{56,48},{64,5... | collective-permute-start | bytes 1204232 | tf_op jit(solution)/shard_map/ppermute | solution.py:26
  306.5 11.3 %collective-permute-start.12 = (bf16[224,896]{1,0:T(8,128)(2,1)S(1)}, bf16[224,896]{1,0:T(8,128)(2,1)}, u32[]{:S(2)}, u32[]{:S(2)}) collective-permute-start(bf16[224,896]{1,0:T(8,128)(2,1)S(1)} %collective-permute-done.11), channel_id=1, source_target_pairs={{0,8},{8,16},{16,24},{24,32},{32,40},{40,48},{48,56},{56,64},{64,7... | collective-permute-start | bytes 1204232 | tf_op jit(solution)/shard_map/ppermute | solution.py:24
  306.8 11.9 %collective-permute-start.19 = (bf16[224,896]{1,0:T(8,128)(2,1)}, bf16[224,896]{1,0:T(8,128)(2,1)}, u32[]{:S(2)}, u32[]{:S(2)}) collective-permute-start(bf16[224,896]{1,0:T(8,128)(2,1)} %collective-permute-done.18), channel_id=1, source_target_pairs={{0,120},{8,0},{16,8},{24,16},{32,24},{40,32},{48,40},{56,48},{64,5... | collective-permute-start | bytes 1204232 | tf_op jit(solution)/shard_map/ppermute | solution.py:26
  317.8 11.5 %collective-permute-start.13 = (bf16[224,896]{1,0:T(8,128)(2,1)}, bf16[224,896]{1,0:T(8,128)(2,1)}, u32[]{:S(2)}, u32[]{:S(2)}) collective-permute-start(bf16[224,896]{1,0:T(8,128)(2,1)} %collective-permute-done.12), channel_id=1, source_target_pairs={{0,8},{8,16},{16,24},{24,32},{32,40},{40,48},{48,56},{56,64},{64,7... | collective-permute-start | bytes 1204232 | tf_op jit(solution)/shard_map/ppermute | solution.py:24
  317.8 26.4 %copy-start.8 = (bf16[224,896]{1,0:T(8,128)(2,1)S(1)}, bf16[224,896]{1,0:T(8,128)(2,1)}, u32[]{:S(2)}) copy-start(bf16[224,896]{1,0:T(8,128)(2,1)} %copy-done.7) | copy-start | bytes 1204228
  318.7 29.8 %collective-permute-start.20 = (bf16[224,896]{1,0:T(8,128)(2,1)}, bf16[224,896]{1,0:T(8,128)(2,1)S(1)}, u32[]{:S(2)}, u32[]{:S(2)}) collective-permute-start(bf16[224,896]{1,0:T(8,128)(2,1)} %collective-permute-done.19), channel_id=1, source_target_pairs={{0,120},{8,0},{16,8},{24,16},{32,24},{40,32},{48,40},{56,48},{64,5... | collective-permute-start | bytes 1204232 | tf_op jit(solution)/shard_map/ppermute | solution.py:26
  459.2 63.7 %copy-start.20 = (f32[448]{0:T(512)S(1)}, f32[448]{0:T(512)}, u32[]{:S(2)}) copy-start(f32[448]{0:T(512)} %param.43) | copy-start | bytes 5380
  461.0 65.9 %copy-start.1 = (bf16[448,3584]{1,0:T(8,128)(2,1)S(1)}, bf16[448,3584]{1,0:T(8,128)(2,1)}, u32[]{:S(2)}) copy-start(bf16[448,3584]{1,0:T(8,128)(2,1)} %param.37) | copy-start | bytes 9633796
  (20 other events, 243.3 us)
Sparse Core Ops, SparseCore 0:
  29.2 88.2 all-gather.9
  227.9 90.6 all-reduce.1
  320.7 61.7 all-gather.5
  384.5 61.5 all-gather.7
  455.2 46.9 reduce-scatter.3
